TPU v7x, 32 devices: a whole 2x2x4 slice. The times are simulated.
32 devices in a mesh: cfg: 2 (over core), seq: 8 (over z, x), wt: 2 (over y).
Axes of the slice: x: 2, y: 2, z: 4, core: 2. Of those that a mesh axis runs over, the one named last changes fastest.
Arguments:
- hidden: bfloat16 [2, 1280, 5120], P('cfg', 'seq'), may hold values from -1.5 to 1.5
- latent: float32 [1280, 64], P('seq', 'cfg'), may hold values from -6 to 6
- tenant_lengths: int32 [4], replicated, may hold values from 1 to 960, 1280 in all
- grid_positions: int32 [1280, 3], P('seq'), may hold values from 0 to 47
- text_kv: bfloat16 [2, 2, 2048, 3072], P(None, 'cfg', None, 'wt'), may hold values from -6 to 6
- text_lengths: int32 [2, 4], P('cfg'), may hold values from 1 to 512
- w_query: bfloat16 [5120, 3072], P(('cfg', 'seq'), 'wt'), may hold values from -0.078125 to 0.078125
- w_key: bfloat16 [5120, 3072], P(('cfg', 'seq'), 'wt'), may hold values from -0.078125 to 0.078125
- w_value: bfloat16 [5120, 3072], P(('cfg', 'seq'), 'wt'), may hold values from -0.078125 to 0.078125
- w_out: bfloat16 [5120, 3072], P(('cfg', 'seq'), 'wt'), may hold values from -0.109375 to 0.109375
- w_cross_query: bfloat16 [5120, 3072], P(('cfg', 'seq'), 'wt'), may hold values from -0.078125 to 0.078125
- w_cross_out: bfloat16 [5120, 3072], P(('cfg', 'seq'), 'wt'), may hold values from -0.109375 to 0.109375
- w_head: bfloat16 [5120, 64], replicated, may hold values from -0.078125 to 0.078125
- guidance: float32 [1], replicated, may hold values from 3 to 7
- step_size: float32 [1], replicated, may hold values from -0.3 to -0.05
Outputs:
- hidden_out: bfloat16 [2, 1280, 5120], P('cfg', 'seq', 'wt')
- latent_next: float32 [1280, 64], P('seq', 'cfg')
Inputs may be any that keep to these rules, and one draw needn't show every extreme that they name: `tenant_lengths`: the lengths sum to 1280; the largest is exactly 960.
All inputs are finite; a program needn't handle non-finite values.
Results may differ from a plain program's by a relative error of at most 0.013.
Values may be sent and summed in bfloat16 or wider, within the bound.
A program may use at most 192 MiB of HBM per device.

v0:
```python
import math
import jax
import jax.numpy as jnp
from jax import lax
from jax.sharding import PartitionSpec as P

HD = 128
TEXT = 512
TENANTS = 4
epsilon = 1e-06


def partner_2(block, axis, distance):
    count = lax.axis_size(axis)
    route = []
    for low in range(count):
        high = low | 1 << distance
        if high != low and high < count:
            route += [(low, high), (high, low)]
    return lax.ppermute(block, axis, route)


def layer_norm(inputs):
    average = jnp.mean(inputs, axis=-1, keepdims=True)
    centred = inputs - average
    variance = jnp.mean(centred * centred, axis=-1, keepdims=True)
    return centred * lax.rsqrt(variance + epsilon)


def head_norm(inputs, head_dim):
    shaped = inputs.reshape(inputs.shape[:-1] + (inputs.shape[-1] // head_dim, head_dim))
    return shaped * lax.rsqrt(jnp.mean(shaped * shaped, axis=-1, keepdims=True) + epsilon)


def rotary(inputs, grid):
    head_dim = inputs.shape[-1]
    sixth_part = head_dim // 6
    angle_parts = []
    for dim_index, span_width in enumerate(
        (head_dim - 4 * sixth_part, 2 * sixth_part, 2 * sixth_part)
    ):
        exponent = jnp.arange(0, span_width, 2).astype(jnp.float32) / span_width
        frequency = 1.0 / 10000.0**exponent
        angle_parts.append(
            grid[:, dim_index : dim_index + 1].astype(jnp.float32) * frequency[None, :]
        )
    angles = jnp.concatenate(angle_parts, axis=1)[:, None, :]
    paired = inputs.reshape(inputs.shape[:-1] + (head_dim // 2, 2))
    even_part = paired[..., 0]
    odd_part = paired[..., 1]
    cosine = jnp.cos(angles)
    sinus = jnp.sin(angles)
    rotated = jnp.stack(
        [even_part * cosine - odd_part * sinus, even_part * sinus + odd_part * cosine], axis=-1
    )
    return rotated.reshape(inputs.shape)


def add_block(queries, keys, values, allowed):
    score_scale = 1.0 / math.sqrt(queries.shape[-1])
    scores = (
        jnp.einsum("qhd,khd->qhk", queries, keys, preferred_element_type=jnp.float32) * score_scale
    )
    weights = jnp.where(allowed[:, None, :], jnp.exp(scores), 0.0).astype(jnp.bfloat16)
    summed = jnp.einsum("qhk,khd->qhd", weights, values, preferred_element_type=jnp.float32)
    totals = jnp.sum(weights.astype(jnp.float32), axis=2)
    return (summed, totals)


def project_rows(normed, weight):
    return jnp.dot(
        normed,
        lax.all_gather(weight, ("cfg", "seq"), axis=0, tiled=True),
        preferred_element_type=jnp.float32,
    )


def project_out(mixed, weight):
    terms = lax.dot_general(
        mixed,
        lax.all_gather(weight, ("cfg", "seq"), axis=0, tiled=True),
        (((1,), (1,)), ((), ())),
        preferred_element_type=jnp.float32,
    )
    return lax.psum(terms.astype(jnp.bfloat16), "wt").astype(jnp.float32)


def on_device(
    hidden,
    latent,
    tenant_lengths,
    grid_positions,
    text_kv,
    text_lengths,
    w_query,
    w_key,
    w_value,
    w_out,
    w_cross_query,
    w_cross_out,
    w_head,
    guidance,
    step_size,
):
    tok_rows = hidden.shape[1]
    model_width = hidden.shape[2]
    local_cols = w_query.shape[1]
    heads_here = local_cols // HD
    seq_index = lax.axis_index("seq")
    ends = jnp.cumsum(tenant_lengths)

    def tenant_of(indices):
        return jnp.sum((indices[:, None] >= ends[None, :]).astype(jnp.int32), axis=1)

    my_tenant = tenant_of(seq_index * tok_rows + jnp.arange(tok_rows, dtype=jnp.int32))
    state = hidden[0].astype(jnp.float32)
    normed = layer_norm(state).astype(jnp.bfloat16)
    joined_weight = jnp.concatenate([w_query, w_key, w_value], axis=1)
    projected = project_rows(normed, joined_weight)
    queries = rotary(head_norm(projected[:, :local_cols], HD), grid_positions).astype(jnp.bfloat16)
    keys = rotary(head_norm(projected[:, local_cols : 2 * local_cols], HD), grid_positions).astype(
        jnp.bfloat16
    )
    keys = keys.reshape(tok_rows, local_cols)
    values = projected[:, 2 * local_cols :].astype(jnp.bfloat16)
    key_piece = lax.all_gather(keys, "seq", axis=0, tiled=True)
    value_piece = lax.all_gather(values, "seq", axis=0, tiled=True)
    piece_rows = key_piece.shape[0]
    key_tenant = tenant_of(jnp.arange(piece_rows, dtype=jnp.int32))
    allowed = my_tenant[:, None] == key_tenant[None, :]
    summed, totals = add_block(
        queries,
        key_piece.reshape(piece_rows, heads_here, HD),
        value_piece.reshape(piece_rows, heads_here, HD),
        allowed,
    )
    mixed = (summed / totals[..., None]).astype(jnp.bfloat16).reshape(tok_rows, local_cols)
    state = state + project_out(mixed, w_out)
    normed = layer_norm(state).astype(jnp.bfloat16)
    cross_queries = head_norm(project_rows(normed, w_cross_query), HD).astype(jnp.bfloat16)
    text_keys = head_norm(text_kv[0, 0].astype(jnp.float32), HD).astype(jnp.bfloat16)
    text_values = text_kv[1, 0].reshape(-1, heads_here, HD)
    text_index = jnp.arange(text_kv.shape[2], dtype=jnp.int32)
    text_tenant = text_index // TEXT
    text_slot = text_index % TEXT
    tenant_table = text_tenant[:, None] == jnp.arange(TENANTS, dtype=jnp.int32)[None, :]
    live_length = jnp.sum(jnp.where(tenant_table, text_lengths[0][None, :], 0), axis=1)
    allowed = (my_tenant[:, None] == text_tenant[None, :]) & (text_slot < live_length)[None, :]
    cross_summed, cross_totals = add_block(cross_queries, text_keys, text_values, allowed)
    cross_mixed = (
        (cross_summed / cross_totals[..., None]).astype(jnp.bfloat16).reshape(tok_rows, local_cols)
    )
    state = state + project_out(cross_mixed, w_cross_out)
    velocity = jnp.dot(
        layer_norm(state).astype(jnp.bfloat16), w_head, preferred_element_type=jnp.float32
    )
    half_index = lax.axis_index("cfg")
    channel_half = latent.shape[1]
    outgoing = lax.dynamic_slice_in_dim(velocity, (1 - half_index) * channel_half, channel_half, 1)
    partner = partner_2(outgoing, "cfg", 0)
    own_part = lax.dynamic_slice_in_dim(velocity, half_index * channel_half, channel_half, 1)
    conditional = jnp.where(half_index == 0, own_part, partner)
    null_text = jnp.where(half_index == 0, partner, own_part)
    latent_next = latent + step_size[0] * (null_text + guidance[0] * (conditional - null_text))
    slice_width = model_width // lax.axis_size("wt")
    hidden_out = lax.dynamic_slice_in_dim(
        state.astype(jnp.bfloat16), lax.axis_index("wt") * slice_width, slice_width, 1
    )
    return (hidden_out[None], latent_next)


def solution(mesh):
    return jax.shard_map(
        on_device,
        mesh=mesh,
        in_specs=(
            P("cfg", "seq", None),
            P("seq", "cfg"),
            P(),
            P("seq", None),
            P(None, "cfg", None, "wt"),
            P("cfg", None),
            P(("cfg", "seq"), "wt"),
            P(("cfg", "seq"), "wt"),
            P(("cfg", "seq"), "wt"),
            P(("cfg", "seq"), "wt"),
            P(("cfg", "seq"), "wt"),
            P(("cfg", "seq"), "wt"),
            P(),
            P(),
            P(),
        ),
        out_specs=(P("cfg", "seq", "wt"), P("seq", "cfg")),
        check_vma=False,
    )
```

profile of v0, /device:TPU:0, one launch (start us, length us, event | category | flops | bytes accessed | tf_op | source)
XLA Modules:
  0.0 949.5 jit_solution(14154485433411646982)
XLA Ops:
  7.2 3.7 pad_maximum_fusion
  12.4 233.7 %all-gather.7.cloned.1.call-done = bf16[5120,4608]{1,0:T(8,128)(2,1)} async-done(((bf16[320,4608]{1,0:T(8,128)(2,1)}), bf16[5120,4608]{1,0:T(8,128)(2,1)}) %all-gather.7.cloned.1.call-update) | async-done | bytes 47185936 | tf_op jit(solution)/shard_map/all_gather | solution.py:73
  246.1 20.1 %fusion.18 = f32[160,4608]{1,0:T(8,128)} fusion(bf16[5120,4608]{1,0:T(8,128)(2,1)} %all-gather.7.cloned.1.call-done, bf16[1,160,5120]{2,1,0:T(8,128)(2,1)S(1)} %copy-done.1, f32[160]{0:T(256)S(1)} %add_rsqrt_fusion.6, f32[160]{0:T(256)S(1)} %broadcast_multiply_fusion.7), kind=kOutput, calls=%fused_computation.31 | convolution fusion | flops 7553024000 | bytes 51774720 | tf_op jit(solution)/shard_map/dot_general | solution.py:71
  266.2 3.3 slice_multiply_fusion
  269.5 2.8 copy.72
  272.3 3.0 reshape.338
  275.3 2.8 copy.76
  278.2 3.0 reshape.340
  288.6 3.2 broadcast_multiply_fusion
  291.8 5.2 subtract_convert_fusion
  297.0 2.8 pad_maximum_fusion.1
  299.9 3.0 convert_element_type.123
  308.3 4.0 pad_maximum_fusion.2
  314.6 60.7 %all-gather.11.cloned.1.call-done = bf16[1280,1536]{1,0:T(8,128)(2,1)} async-done(((bf16[160,1536]{1,0:T(8,128)(2,1)}), bf16[1280,1536]{1,0:T(8,128)(2,1)}) %all-gather.11.cloned.1.call-update) | async-done | bytes 3932176 | tf_op jit(solution)/shard_map/all_gather | solution.py:126
  375.3 6.3 copy.75
  381.6 64.4 %all-gather.9.cloned.1.call-done = bf16[1280,1536]{1,0:T(8,128)(2,1)} async-done(((bf16[160,1536]{1,0:T(8,128)(2,1)}), bf16[1280,1536]{1,0:T(8,128)(2,1)}) %all-gather.9.cloned.1.call-update) | async-done | bytes 3932176 | tf_op jit(solution)/shard_map/all_gather | solution.py:127
  445.9 6.2 copy.71
  452.1 5.6 convert_reduce_fusion.1
  459.2 107.6 %all-gather.13.cloned.1.call-done = bf16[5120,1536]{1,0:T(8,128)(2,1)} async-done(((bf16[320,1536]{1,0:T(8,128)(2,1)}), bf16[5120,1536]{1,0:T(8,128)(2,1)}) %all-gather.13.cloned.1.call-update) | async-done | bytes 15728656 | tf_op jit(solution)/shard_map/all_gather | solution.py:81
  566.7 11.9 %convolution_convert_fusion.1 = bf16[160,5120]{1,0:T(8,128)(2,1)} fusion(bf16[5120,1536]{1,0:T(8,128)(2,1)} %all-gather.13.cloned.1.call-done, bf16[12,20,8,128]{3,2,1,0:T(8,128)(2,1)S(1)} %fusion.28), kind=kOutput, calls=%fused_computation.13 | convolution fusion | flops 2517401600 | bytes 17858560 | tf_op jit(solution)/shard_map/dot_general | solution.py:79
  580.0 10.6 %fusion.47 = (bf16[1,1,2048,1536]{3,2,1,0:T(8,128)(2,1)}, bf16[1,1,2048,1536]{3,2,1,0:T(8,128)(2,1)}) fusion(bf16[2,1,2048,1536]{3,2,1,0:T(8,128)(2,1)} %param.19), kind=kLoop, calls=%fused_computation.109 | loop fusion | bytes 25165824 | tf_op jit(solution)/shard_map/slice | solution.py:142
  590.6 8.7 copy.95
  599.4 8.8 copy.96
  608.3 4.7 fusion.1
  614.0 15.8 %all-reduce.3.cloned.1.call-done = bf16[160,5120]{1,0:T(8,128)(2,1)} async-done(((bf16[160,5120]{1,0:T(8,128)(2,1)}), bf16[160,5120]{1,0:T(8,128)(2,1)}) %all-reduce.3.cloned.1.call-update) | async-done | bytes 1638416 | tf_op jit(solution)/shard_map/psum | solution.py:85
  632.7 119.8 %all-gather.15.cloned.1.call-done = bf16[5120,1536]{1,0:T(8,128)(2,1)} async-done(((bf16[320,1536]{1,0:T(8,128)(2,1)}), bf16[5120,1536]{1,0:T(8,128)(2,1)}) %all-gather.15.cloned.1.call-update) | async-done | bytes 15728656 | tf_op jit(solution)/shard_map/all_gather | solution.py:73
  752.5 7.6 fusion.16
  765.3 7.7 convert_reduce_fusion
  775.3 98.3 %all-gather.17.cloned.1.call-done = bf16[5120,1536]{1,0:T(8,128)(2,1)} async-done(((bf16[320,1536]{1,0:T(8,128)(2,1)}), bf16[5120,1536]{1,0:T(8,128)(2,1)}) %all-gather.17.cloned.1.call-update) | async-done | bytes 15728656 | tf_op jit(solution)/shard_map/all_gather | solution.py:81
  873.5 11.9 %convolution_convert_fusion = bf16[160,5120]{1,0:T(8,128)(2,1)} fusion(bf16[5120,1536]{1,0:T(8,128)(2,1)} %all-gather.17.cloned.1.call-done, bf16[12,20,8,128]{3,2,1,0:T(8,128)(2,1)S(1)} %fusion.29), kind=kOutput, calls=%fused_computation.12 | convolution fusion | flops 2517401600 | bytes 17858560 | tf_op jit(solution)/shard_map/dot_general | solution.py:79
  886.7 49.9 %all-reduce.5.cloned.1.call-done = bf16[160,5120]{1,0:T(8,128)(2,1)} async-done(((bf16[160,5120]{1,0:T(8,128)(2,1)}), bf16[160,5120]{1,0:T(8,128)(2,1)}) %all-reduce.5.cloned.1.call-update) | async-done | bytes 1638416 | tf_op jit(solution)/shard_map/psum | solution.py:85
  936.7 2.6 fusion.46
  (91 shorter events, 33.8 us)
Async XLA Ops:
  7.2 932.6 %copy-start = (bf16[5120,64]{0,1:T(8,128)(2,1)S(1)}, bf16[5120,64]{0,1:T(8,128)(2,1)}, u32[]{:S(2)}) copy-start(bf16[5120,64]{0,1:T(8,128)(2,1)} %param.27) | copy-start | bytes 1966084
  7.2 3.9 copy-start.6
  7.2 4.3 copy-start.1
  7.2 238.9 %all-gather.7.cloned.1.call-start = ((), (), s32[]{:S(2)}) async-start(), calls=%async_computation | async-start | bytes 50135040 | tf_op jit(solution)/shard_map/all_gather | solution.py:73
  11.0 364.3 %all-gather.11.cloned.1.call-start = ((), (), s32[]{:S(2)}) async-start(), calls=%async_computation.2 | async-start | bytes 4423680 | tf_op jit(solution)/shard_map/all_gather | solution.py:126
  299.9 7.9 copy-start.8
  305.0 140.9 %all-gather.9.cloned.1.call-start = ((), (), s32[]{:S(2)}) async-start(), calls=%async_computation.1 | async-start | bytes 4423680 | tf_op jit(solution)/shard_map/all_gather | solution.py:127
  307.1 259.6 %all-gather.13.cloned.1.call-start = ((), (), s32[]{:S(2)}) async-start(), calls=%async_computation.3 | async-start | bytes 16711680 | tf_op jit(solution)/shard_map/all_gather | solution.py:81
  307.7 322.1 %all-reduce.3.cloned.1.call-start = ((), (), s32[]{:S(2)}) async-start(), calls=%async_computation.4 | async-start | bytes 3276800 | tf_op jit(solution)/shard_map/psum | solution.py:85
  452.1 5.6 copy-start.3
  578.6 173.9 %all-gather.15.cloned.1.call-start = ((), (), s32[]{:S(2)}) async-start(), calls=%async_computation.5 | async-start | bytes 16711680 | tf_op jit(solution)/shard_map/all_gather | solution.py:73
  579.2 294.3 %all-gather.17.cloned.1.call-start = ((), (), s32[]{:S(2)}) async-start(), calls=%async_computation.6 | async-start | bytes 16711680 | tf_op jit(solution)/shard_map/all_gather | solution.py:81
  580.0 356.7 %all-reduce.5.cloned.1.call-start = ((), (), s32[]{:S(2)}) async-start(), calls=%async_computation.7 | async-start | bytes 3276800 | tf_op jit(solution)/shard_map/psum | solution.py:85
  599.4 8.8 copy-start.7
  629.9 2.1 copy-start.2
  761.3 4.0 copy-start.4
  763.4 9.6 %slice-start = ((s8[6291456]{0:T(1024)(128)(4,1)}), s8[4194304]{0:T(1024)(128)(4,1)S(1)}, s32[]{:S(2)}) async-start(s8[6291456]{0:T(1024)(128)(4,1)} %bitcast.95), calls=%async_computation.8 | async-start | bytes 8388608
  765.3 7.7 slice-start.1
  939.8 2.1 copy-start.5
  940.6 1.3 collective-permute-start
Sparse Core Ops, SparseCore 0:
  11.1 234.9 all-gather.6
  305.1 70.0 all-gather.10
  377.5 68.4 all-gather.8
  448.0 118.6 all-gather.12
  578.7 51.0 all-reduce.2
  632.2 120.2 all-gather.14
  755.0 118.4 all-gather.16
  885.5 51.0 all-reduce.4
where the time goes:
time: 959 us; the launch traced here: 950 us
  waiting for transfers between devices  752 us (78%)
  matrix products  69 us (7%)
  local copies, waits for them, and re-layouts  68.1 us (7%)
  other arithmetic  43.8 us (5%)
  between operations  16 us (2%)
    all_gather x2, waiting for transfers between devices, project_rows(): lax.all_gather(weight, ('cfg', 'seq'), axis=0, tiled=True)  354 us
    all_gather x2, waiting for transfers between devices, project_out(): lax.all_gather(weight, ('cfg', 'seq'), axis=0, tiled=True)  206 us
    psum x2, waiting for transfers between devices, project_out(): return lax.psum(terms.astype(jnp.bfloat16), 'wt').astype(jnp.float32)  65.8 us
    all_gather x1, waiting for transfers between devices, on_device(): value_piece = lax.all_gather(values, 'seq', axis=0, tiled=True)  64.4 us
    all_gather x1, waiting for transfers between devices, on_device(): key_piece = lax.all_gather(keys, 'seq', axis=0, tiled=True)  60.7 us
    dot_general x2, matrix products, project_rows(): jnp.dot(normed, lax.all_gather(weight, ('cfg', 'seq'), axis=0, tiled=True...  27.7 us
    dot_general x2, matrix products, project_out(): lax.dot_general(mixed, lax.all_gather(weight, ('cfg', 'seq'), axis=0, til...  23.7 us
  transfers between devices with their start and end apart: 9, of which 9 were waited for; matrix products, arithmetic and copies ran while one was open for 9% of the time, Pallas kernels for 0%

commit v1 on v0

--- a/solution.py
+++ b/solution.py
@@ -8,6 +8,24 @@
 TEXT = 512
 TENANTS = 4
 epsilon = 1e-06
+
+
+def gather_around(array, axis, dim):
+    ways, here, step = (lax.axis_size(axis), lax.axis_index(axis), array.shape[dim])
+    shape = [n * ways if d == dim else n for d, n in enumerate(array.shape)]
+    full = lax.dynamic_update_slice_in_dim(
+        jnp.zeros(shape, array.dtype), array, here * step, axis=dim
+    )
+    going_up = going_down = array
+    for far in range(1, ways // 2 + 1):
+        going_up = lax.ppermute(going_up, axis, [(d, (d + 1) % ways) for d in range(ways)])
+        full = lax.dynamic_update_slice_in_dim(full, going_up, (here - far) % ways * step, axis=dim)
+        if 2 * far < ways:
+            going_down = lax.ppermute(going_down, axis, [(d, (d - 1) % ways) for d in range(ways)])
+            full = lax.dynamic_update_slice_in_dim(
+                full, going_down, (here + far) % ways * step, axis=dim
+            )
+    return full
 
 
 def partner_2(block, axis, distance):
@@ -123,7 +141,7 @@
     )
     keys = keys.reshape(tok_rows, local_cols)
     values = projected[:, 2 * local_cols :].astype(jnp.bfloat16)
-    key_piece = lax.all_gather(keys, "seq", axis=0, tiled=True)
+    key_piece = gather_around(keys, "seq", 0)
     value_piece = lax.all_gather(values, "seq", axis=0, tiled=True)
     piece_rows = key_piece.shape[0]
     key_tenant = tenant_of(jnp.arange(piece_rows, dtype=jnp.int32))

time: 959 us -> 895 us (0.933)
  waiting for transfers between devices: 752 us -> 596 us
  local copies, waits for them, and re-layouts: 68.1 us -> 141 us
  starting transfers between devices: 0.39 us -> 17.1 us
    all_gather x2, waiting for transfers between devices: 206 us -> 117 us  [project_out(): lax.all_gather(weight, ('cfg', 'seq'), axis=0, tiled=True)]
    dynamic_update_slice x0 -> x8, local copies, waits for them, and re-layouts: none -> 68.3 us  [the longest x4 33.7 us: gather_around(): lax.dynamic_update_slice_in_dim(full, going_up, (here - far) % ways * ste...]
    all_gather x1, waiting for transfers between devices: 64.4 us -> 0.01 us  [on_device(): value_piece = lax.all_gather(values, 'seq', axis=0, tiled=True)]
    all_gather x1 -> x0, waiting for transfers between devices: 60.7 us -> none  [on_device(): key_piece = lax.all_gather(keys, 'seq', axis=0, tiled=True)]
    ppermute x0 -> x7, waiting for transfers between devices: none -> 54.2 us  [the longest x4 54.2 us: gather_around(): lax.ppermute(going_up, axis, [(d, (d + 1) % ways) for d in range(ways)])]
    ppermute x0 -> x7, starting transfers between devices: none -> 16.5 us  [the longest x3 11.3 us: gather_around(): lax.ppermute(going_down, axis, [(d, (d - 1) % ways) for d in range(ways)])]
  transfers between devices with their start and end apart: 9 -> 15, of which waited for: 9 -> 10; matrix products, arithmetic and copies ran while one was open for 9% -> 23% of each run, Pallas kernels for 0% -> 0%
where the time goes in v1:
time: 895 us; the launch traced here: 888 us
  waiting for transfers between devices  596 us (67%)
  local copies, waits for them, and re-layouts  141 us (16%)
  matrix products  74.5 us (8%)
  other arithmetic  43.7 us (5%)
  starting transfers between devices  17.1 us (2%)
  between operations  16 us (2%)
    all_gather x2, waiting for transfers between devices, project_rows(): lax.all_gather(weight, ('cfg', 'seq'), axis=0, tiled=True)  354 us
    all_gather x2, waiting for transfers between devices, project_out(): lax.all_gather(weight, ('cfg', 'seq'), axis=0, tiled=True)  117 us
    psum x2, waiting for transfers between devices, project_out(): return lax.psum(terms.astype(jnp.bfloat16), 'wt').astype(jnp.float32)  69 us
    ppermute x4, waiting for transfers between devices, gather_around(): lax.ppermute(going_up, axis, [(d, (d + 1) % ways) for d in range(ways)])  54.2 us
    dynamic_update_slice x4, local copies, waits for them, and re-layouts, gather_around(): lax.dynamic_update_slice_in_dim(full, going_up, (here - far) % ways * ste...  33.7 us
    dot_general x2, matrix products, project_rows(): jnp.dot(normed, lax.all_gather(weight, ('cfg', 'seq'), axis=0, tiled=True...  27.6 us
    dynamic_update_slice x3, local copies, waits for them, and re-layouts, gather_around(): lax.dynamic_update_slice_in_dim(full, going_down, (here + far) % ways * s...  26.7 us
    dot_general x2, matrix products, project_out(): lax.dot_general(mixed, lax.all_gather(weight, ('cfg', 'seq'), axis=0, til...  23.7 us
  transfers between devices with their start and end apart: 15, of which 10 were waited for; matrix products, arithmetic and copies ran while one was open for 23% of the time, Pallas kernels for 0%

profile of v1, /device:TPU:0, one launch (start us, length us, event | category | flops | bytes accessed | tf_op | source)
XLA Modules:
  0.0 888.5 jit_solution(15406728507043232936)
XLA Ops:
  12.0 234.1 %all-gather.6.cloned.1.call-done = bf16[5120,4608]{1,0:T(8,128)(2,1)} async-done(((bf16[320,4608]{1,0:T(8,128)(2,1)}), bf16[5120,4608]{1,0:T(8,128)(2,1)}) %all-gather.6.cloned.1.call-update) | async-done | bytes 47185936 | tf_op jit(solution)/shard_map/all_gather | solution.py:91
  246.1 20.1 %fusion.18 = f32[160,4608]{1,0:T(8,128)} fusion(bf16[5120,4608]{1,0:T(8,128)(2,1)} %all-gather.6.cloned.1.call-done, bf16[1,160,5120]{2,1,0:T(8,128)(2,1)S(1)} %copy-done.1, f32[160]{0:T(256)S(1)} %add_rsqrt_fusion.6, f32[160]{0:T(256)S(1)} %broadcast_multiply_fusion.7), kind=kOutput, calls=%fused_computation.31 | convolution fusion | flops 7553024000 | bytes 51774720 | tf_op jit(solution)/shard_map/dot_general | solution.py:89
  295.6 5.1 subtract_convert_fusion
  311.5 29.0 %collective-permute-done = bf16[160,1536]{1,0:T(8,128)(2,1)S(1)} collective-permute-done((bf16[160,1536]{1,0:T(8,128)(2,1)}, bf16[160,1536]{1,0:T(8,128)(2,1)S(1)}, u32[]{:S(2)}, u32[]{:S(2)}) %collective-permute-start) | collective-permute-done | bytes 491552 | tf_op jit(solution)/shard_map/ppermute | solution.py:21
  346.0 19.2 %collective-permute-done.2 = bf16[160,1536]{1,0:T(8,128)(2,1)} collective-permute-done((bf16[160,1536]{1,0:T(8,128)(2,1)S(1)}, bf16[160,1536]{1,0:T(8,128)(2,1)}, u32[]{:S(2)}, u32[]{:S(2)}) %collective-permute-start.2) | collective-permute-done | bytes 491552 | tf_op jit(solution)/shard_map/ppermute | solution.py:21
  367.0 5.2 collective-permute-start.5
  372.2 6.0 collective-permute-done.4
  378.9 4.4 pad_maximum_fusion.2
  388.4 7.9 dynamic_update_slice.24
  397.6 8.2 dynamic_update_slice.25
  407.1 8.9 dynamic_update_slice.26
  417.3 8.7 dynamic_update_slice.27
  427.3 9.0 %dynamic_update_slice.28 = bf16[1280,1536]{0,1:T(8,128)(2,1)} dynamic-update-slice(bf16[1280,1536]{0,1:T(8,128)(2,1)} %dynamic_update_slice.27, bf16[160,1536]{0,1:T(8,128)(2,1)S(1)} %copy.93, s32[]{:T(128)S(6)} %select_n.121, s32[]{:T(128)} %constant.124.clone.1) | dynamic-update-slice | bytes 983044 | tf_op jit(solution)/shard_map/dynamic_update_slice | solution.py:25
  437.5 8.9 %dynamic_update_slice.29 = bf16[1280,1536]{0,1:T(8,128)(2,1)} dynamic-update-slice(bf16[1280,1536]{0,1:T(8,128)(2,1)} %dynamic_update_slice.28, bf16[160,1536]{0,1:T(8,128)(2,1)S(1)} %copy.94, s32[]{:T(128)S(6)} %select_n.123, s32[]{:T(128)} %constant.124.clone.1) | dynamic-update-slice | bytes 983044 | tf_op jit(solution)/shard_map/dynamic_update_slice | solution.py:22
  447.8 8.8 dynamic_update_slice.30
  457.9 8.0 dynamic_update_slice.31
  465.9 7.5 convert_reduce_fusion.1
  473.4 6.5 copy.85
  480.0 5.0 fusion.28
  485.0 18.4 %all-gather.10.cloned.1.call-done = bf16[5120,1536]{1,0:T(8,128)(2,1)} async-done(((bf16[320,1536]{1,0:T(8,128)(2,1)}), bf16[5120,1536]{1,0:T(8,128)(2,1)}) %all-gather.10.cloned.1.call-update) | async-done | bytes 15728656 | tf_op jit(solution)/shard_map/all_gather | solution.py:99
  503.4 11.9 %convolution_convert_fusion.1 = bf16[160,5120]{1,0:T(8,128)(2,1)} fusion(bf16[5120,1536]{1,0:T(8,128)(2,1)} %all-gather.10.cloned.1.call-done, bf16[12,20,8,128]{3,2,1,0:T(8,128)(2,1)S(1)} %fusion.28), kind=kOutput, calls=%fused_computation.13 | convolution fusion | flops 2517401600 | bytes 17858560 | tf_op jit(solution)/shard_map/dot_general | solution.py:97
  516.5 10.3 %fusion.47 = (bf16[1,1,2048,1536]{3,2,1,0:T(8,128)(2,1)}, bf16[1,1,2048,1536]{3,2,1,0:T(8,128)(2,1)}) fusion(bf16[2,1,2048,1536]{3,2,1,0:T(8,128)(2,1)} %param.19), kind=kLoop, calls=%fused_computation.109 | loop fusion | bytes 25165824 | tf_op jit(solution)/shard_map/slice | solution.py:160
  526.9 8.7 copy.116
  535.6 8.8 copy.117
  544.6 4.3 fusion.1
  549.9 19.1 %all-reduce.3.cloned.1.call-done = bf16[160,5120]{1,0:T(8,128)(2,1)} async-done(((bf16[160,5120]{1,0:T(8,128)(2,1)}), bf16[160,5120]{1,0:T(8,128)(2,1)}) %all-reduce.3.cloned.1.call-update) | async-done | bytes 1638416 | tf_op jit(solution)/shard_map/psum | solution.py:103
  571.8 119.8 %all-gather.12.cloned.1.call-done = bf16[5120,1536]{1,0:T(8,128)(2,1)} async-done(((bf16[320,1536]{1,0:T(8,128)(2,1)}), bf16[5120,1536]{1,0:T(8,128)(2,1)}) %all-gather.12.cloned.1.call-update) | async-done | bytes 15728656 | tf_op jit(solution)/shard_map/all_gather | solution.py:91
  691.6 7.6 fusion.16
  704.4 7.7 convert_reduce_fusion
  714.3 98.2 %all-gather.14.cloned.1.call-done = bf16[5120,1536]{1,0:T(8,128)(2,1)} async-done(((bf16[320,1536]{1,0:T(8,128)(2,1)}), bf16[5120,1536]{1,0:T(8,128)(2,1)}) %all-gather.14.cloned.1.call-update) | async-done | bytes 15728656 | tf_op jit(solution)/shard_map/all_gather | solution.py:99
  812.4 11.9 %convolution_convert_fusion = bf16[160,5120]{1,0:T(8,128)(2,1)} fusion(bf16[5120,1536]{1,0:T(8,128)(2,1)} %all-gather.14.cloned.1.call-done, bf16[12,20,8,128]{3,2,1,0:T(8,128)(2,1)S(1)} %fusion.29), kind=kOutput, calls=%fused_computation.12 | convolution fusion | flops 2517401600 | bytes 17858560 | tf_op jit(solution)/shard_map/dot_general | solution.py:97
  825.6 49.9 %all-reduce.5.cloned.1.call-done = bf16[160,5120]{1,0:T(8,128)(2,1)} async-done(((bf16[160,5120]{1,0:T(8,128)(2,1)}), bf16[160,5120]{1,0:T(8,128)(2,1)}) %all-reduce.5.cloned.1.call-update) | async-done | bytes 1638416 | tf_op jit(solution)/shard_map/psum | solution.py:103
  (117 shorter events, 85.4 us)
Async XLA Ops:
  7.2 871.6 %copy-start = (bf16[5120,64]{0,1:T(8,128)(2,1)S(1)}, bf16[5120,64]{0,1:T(8,128)(2,1)}, u32[]{:S(2)}) copy-start(bf16[5120,64]{0,1:T(8,128)(2,1)} %param.27) | copy-start | bytes 1966084
  7.2 3.9 copy-start.1
  7.2 238.9 %all-gather.6.cloned.1.call-start = ((), (), s32[]{:S(2)}) async-start(), calls=%async_computation | async-start | bytes 50135040 | tf_op jit(solution)/shard_map/all_gather | solution.py:91
  11.0 462.4 %all-gather.8.cloned.1.call-start = ((), (), s32[]{:S(2)}) async-start(), calls=%async_computation.1 | async-start | bytes 4423680 | tf_op jit(solution)/shard_map/all_gather | solution.py:145
  12.0 257.3 %copy-start.6 = (s32[160,3]{0,1:T(4,128)S(1)}, s32[160,3]{0,1:T(4,128)}, u32[]{:S(2)}) copy-start(s32[160,3]{0,1:T(4,128)} %param.18) | copy-start | bytes 5764
  268.2 235.2 %all-gather.10.cloned.1.call-start = ((), (), s32[]{:S(2)}) async-start(), calls=%async_computation.2 | async-start | bytes 16711680 | tf_op jit(solution)/shard_map/all_gather | solution.py:99
  269.0 300.0 %all-reduce.3.cloned.1.call-start = ((), (), s32[]{:S(2)}) async-start(), calls=%async_computation.3 | async-start | bytes 3276800 | tf_op jit(solution)/shard_map/psum | solution.py:103
  300.6 66.0 %copy-start.8 = (s32[4]{0:T(128)S(1)}, s32[4]{0:T(128)}, u32[]{:S(2)}) copy-start(s32[4]{0:T(128)} %param.17) | copy-start | bytes 52
  306.8 33.7 %collective-permute-start = (bf16[160,1536]{1,0:T(8,128)(2,1)}, bf16[160,1536]{1,0:T(8,128)(2,1)S(1)}, u32[]{:S(2)}, u32[]{:S(2)}) collective-permute-start(bf16[160,1536]{1,0:T(8,128)(2,1)} %copy.88), channel_id=1, source_target_pairs={{0,2},{2,4},{4,6},{6,8},{8,10},{10,12},{12,14},{14,0},{1,3},{3,5},... | collective-permute-start | bytes 1474568 | tf_op jit(solution)/shard_map/ppermute | solution.py:21
  307.7 35.9 %collective-permute-start.1 = (bf16[160,1536]{1,0:T(8,128)(2,1)}, bf16[160,1536]{1,0:T(8,128)(2,1)}, u32[]{:S(2)}, u32[]{:S(2)}) collective-permute-start(bf16[160,1536]{1,0:T(8,128)(2,1)} %copy.88), channel_id=1, source_target_pairs={{0,14},{2,0},{4,2},{6,4},{8,6},{10,8},{12,10},{14,12},{1,15},{3,1}... | collective-permute-start | bytes 1474568 | tf_op jit(solution)/shard_map/ppermute | solution.py:24
  340.5 0.8 copy-start.3
  341.3 23.9 %collective-permute-start.2 = (bf16[160,1536]{1,0:T(8,128)(2,1)S(1)}, bf16[160,1536]{1,0:T(8,128)(2,1)}, u32[]{:S(2)}, u32[]{:S(2)}) collective-permute-start(bf16[160,1536]{1,0:T(8,128)(2,1)S(1)} %collective-permute-done), channel_id=1, source_target_pairs={{0,2},{2,4},{4,6},{6,8},{8,10},{10,12},{12,14},{14,0},{1,3},{3,5},... | collective-permute-start | bytes 1474568 | tf_op jit(solution)/shard_map/ppermute | solution.py:21
  343.6 23.3 %collective-permute-start.3 = (bf16[160,1536]{1,0:T(8,128)(2,1)}, bf16[160,1536]{1,0:T(8,128)(2,1)}, u32[]{:S(2)}, u32[]{:S(2)}) collective-permute-start(bf16[160,1536]{1,0:T(8,128)(2,1)} %collective-permute-done.1), channel_id=1, source_target_pairs={{0,14},{2,0},{4,2},{6,4},{8,6},{10,8},{12,10},{14,12},{1,15},{3,1}... | collective-permute-start | bytes 1474568 | tf_op jit(solution)/shard_map/ppermute | solution.py:24
  365.2 13.1 %collective-permute-start.4 = (bf16[160,1536]{1,0:T(8,128)(2,1)}, bf16[160,1536]{1,0:T(8,128)(2,1)}, u32[]{:S(2)}, u32[]{:S(2)}) collective-permute-start(bf16[160,1536]{1,0:T(8,128)(2,1)} %collective-permute-done.2), channel_id=1, source_target_pairs={{0,2},{2,4},{4,6},{6,8},{8,10},{10,12},{12,14},{14,0},{1,3},{3,5},... | collective-permute-start | bytes 1474568 | tf_op jit(solution)/shard_map/ppermute | solution.py:21
  367.0 79.5 %collective-permute-start.5 = (bf16[160,1536]{1,0:T(8,128)(2,1)}, bf16[160,1536]{1,0:T(8,128)(2,1)}, u32[]{:S(2)}, u32[]{:S(2)}) collective-permute-start(bf16[160,1536]{1,0:T(8,128)(2,1)} %collective-permute-done.3), channel_id=1, source_target_pairs={{0,14},{2,0},{4,2},{6,4},{8,6},{10,8},{12,10},{14,12},{1,15},{3,1}... | collective-permute-start | bytes 1474568 | tf_op jit(solution)/shard_map/ppermute | solution.py:24
  378.3 78.4 %collective-permute-start.6 = (bf16[160,1536]{1,0:T(8,128)(2,1)}, bf16[160,1536]{1,0:T(8,128)(2,1)}, u32[]{:S(2)}, u32[]{:S(2)}) collective-permute-start(bf16[160,1536]{1,0:T(8,128)(2,1)} %collective-permute-done.4), channel_id=1, source_target_pairs={{0,2},{2,4},{4,6},{6,8},{8,10},{10,12},{12,14},{14,0},{1,3},{3,5},... | collective-permute-start | bytes 1474568 | tf_op jit(solution)/shard_map/ppermute | solution.py:21
  515.3 176.3 %all-gather.12.cloned.1.call-start = ((), (), s32[]{:S(2)}) async-start(), calls=%async_computation.4 | async-start | bytes 16711680 | tf_op jit(solution)/shard_map/all_gather | solution.py:91
  515.9 296.5 %all-gather.14.cloned.1.call-start = ((), (), s32[]{:S(2)}) async-start(), calls=%async_computation.5 | async-start | bytes 16711680 | tf_op jit(solution)/shard_map/all_gather | solution.py:99
  516.5 359.1 %all-reduce.5.cloned.1.call-start = ((), (), s32[]{:S(2)}) async-start(), calls=%async_computation.6 | async-start | bytes 3276800 | tf_op jit(solution)/shard_map/psum | solution.py:103
  535.6 8.8 copy-start.7
  568.9 2.1 copy-start.2
  700.4 4.0 copy-start.4
  702.5 9.6 %slice-start = ((s8[6291456]{0:T(1024)(128)(4,1)}), s8[4194304]{0:T(1024)(128)(4,1)S(1)}, s32[]{:S(2)}) async-start(s8[6291456]{0:T(1024)(128)(4,1)} %bitcast.95), calls=%async_computation.7 | async-start | bytes 8388608
  704.4 7.7 slice-start.1
  878.7 2.1 copy-start.5
  879.5 1.3 collective-permute-start.7
Sparse Core Ops, SparseCore 0:
  11.1 234.9 all-gather.5
  268.4 99.4 all-gather.7
  370.1 133.2 all-gather.9
  515.5 53.4 all-reduce.2
  571.3 120.2 all-gather.11
  693.9 118.4 all-gather.13
  824.4 51.0 all-reduce.4
